TPU v7x, 32 devices: a whole 2x2x4 slice. The times are simulated.
32 devices in a mesh: dp: 4 (over y, x), rows: 2 (over core), tm: 4 (over z).
Axes of the slice: x: 2, y: 2, z: 4, core: 2. Of those that a mesh axis runs over, the one named last changes fastest.
Arguments:
- video_cells: bfloat16 [4, 8, 8, 128, 128], P('dp', 'tm', 'rows'), may hold values from -6 to 6
- block_weight: bfloat16 [3, 3, 3, 128, 128], replicated, may hold values from -0.109375 to 0.109375
- down_weight: bfloat16 [3, 3, 3, 128, 256], replicated, may hold values from -0.109375 to 0.109375
- cotangent: bfloat16 [4, 4, 4, 64, 256], P('dp', 'tm', 'rows'), may hold values from -6 to 6
Outputs:
- latents: bfloat16 [4, 4, 4, 64, 256], P('dp', 'tm', 'rows')
- grad_video: bfloat16 [4, 8, 8, 128, 128], P('dp', 'tm', 'rows')
- grad_block: float32 [3, 3, 3, 128, 128], replicated
- grad_down: float32 [3, 3, 3, 128, 256], replicated
All inputs are finite; a program needn't handle non-finite values.
Results may differ from a plain program's by a relative error of at most 0.0055.
Values may be sent and summed in bfloat16 or wider, within the bound.
A program may use at most 64 MiB of HBM per device.

v0:
```python
import jax
import jax.numpy as jnp
from jax import lax
from jax.sharding import PartitionSpec as P


def from_behind(value, axis, steps):
    count = lax.axis_size(axis)
    leading, last = (max(0, -steps), min(count, count - steps))
    return lax.ppermute(value, axis, [(source, source + steps) for source in range(leading, last)])


def with_halo(cells, sides, width):
    for axis, dim in sides:
        count = lax.axis_size(axis)
        ends = count - 1
        head = lax.slice_in_dim(cells, 0, width, axis=dim)
        tail = lax.slice_in_dim(cells, cells.shape[dim] - width, cells.shape[dim], axis=dim)
        cells = jnp.concatenate(
            [
                lax.ppermute(tail, axis, [(i, (i + 1) % count) for i in range(ends)]),
                cells,
                lax.ppermute(head, axis, [((i + 1) % count, i) for i in range(ends)]),
            ],
            axis=dim,
        )
    return cells


def tap_list():
    return [
        (frame_tap, row_tap, column_tap)
        for frame_tap in range(3)
        for row_tap in range(3)
        for column_tap in range(3)
    ]


def plane_list():
    return [(frame_tap, row_tap) for frame_tap in range(3) for row_tap in range(3)]


def parity_taps(parity):
    if parity == 0:
        return [(1, 0)]
    return [(0, 1), (2, 0)]


def frame_edge(tensor, amount, direction):
    portion = tensor[tensor.shape[0] - amount :] if direction == 1 else tensor
    received = from_behind(portion, "tm", direction)
    if direction == 1:
        return jnp.concatenate([received, tensor], axis=0)
    return jnp.concatenate([tensor, received], axis=0)


def row_edge(tensor, direction):
    portion = tensor[:, tensor.shape[1] - 1 :] if direction == 1 else tensor[:, :1]
    received = from_behind(portion, "rows", direction)
    if direction == 1:
        return jnp.concatenate([received, tensor], axis=1)
    return jnp.concatenate([tensor, received], axis=1)


def row_margin(tensor):
    return with_halo(tensor, (("rows", 1),), 1)


def outer_sum(patches, cotangent_part):
    return lax.dot_general(
        patches.reshape(-1, patches.shape[-1]),
        cotangent_part.reshape(-1, cotangent_part.shape[-1]),
        (((0,), (0,)), ((), ())),
        preferred_element_type=jnp.float32,
    )


def local(video_cells, block_weight, down_weight, cotangent):
    channels = video_cells.shape[-1]
    wide_channels = down_weight.shape[-1]
    source = video_cells[0].astype(jnp.float32)
    frames, height, columns = (source.shape[0], source.shape[1], source.shape[2])
    activated = jax.nn.silu(source).astype(jnp.bfloat16)
    padded_a = row_margin(frame_edge(activated, 2, 1))
    padded_a = jnp.pad(padded_a, ((0, 0), (0, 0), (1, 1), (0, 0)))
    branch = jnp.zeros((frames, height, columns, channels), jnp.float32)
    for frame_tap, row_tap in plane_list():
        window = jnp.concatenate(
            [
                padded_a[
                    frame_tap : frame_tap + frames,
                    row_tap : row_tap + height,
                    column_tap : column_tap + columns,
                ]
                for column_tap in range(3)
            ],
            axis=-1,
        )
        branch = branch + jnp.dot(
            window,
            block_weight[frame_tap, row_tap].reshape(3 * channels, channels),
            preferred_element_type=jnp.float32,
        )
    summed = (source + branch).astype(jnp.bfloat16)
    padded_b = row_edge(frame_edge(summed, 1, 1), 1)
    padded_b = jnp.pad(padded_b, ((0, 0), (0, 0), (1, 0), (0, 0)))
    patches_b = jnp.concatenate(
        [
            padded_b[
                frame_tap : frame_tap + frames - 1 : 2,
                row_tap : row_tap + height - 1 : 2,
                column_tap : column_tap + columns - 1 : 2,
            ]
            for frame_tap, row_tap, column_tap in tap_list()
        ],
        axis=-1,
    )
    down_matrix = down_weight.reshape(27 * channels, wide_channels)
    latents = jnp.dot(patches_b, down_matrix, preferred_element_type=jnp.float32).astype(
        jnp.bfloat16
    )
    incoming = cotangent[0]
    grad_down_term = outer_sum(patches_b, incoming)
    extended = row_edge(frame_edge(incoming, 1, -1), -1)
    extended = jnp.pad(extended, ((0, 0), (0, 0), (0, 1), (0, 0)))
    out_frames, out_rows, out_columns = (frames // 2, height // 2, columns // 2)
    parity_parts = []
    for frame_parity in range(2):
        for row_parity in range(2):
            for column_parity in range(2):
                windows = []
                kernels = []
                for frame_tap, frame_shift in parity_taps(frame_parity):
                    for row_tap, row_shift in parity_taps(row_parity):
                        for column_tap, column_shift in parity_taps(column_parity):
                            windows.append(
                                extended[
                                    frame_shift : frame_shift + out_frames,
                                    row_shift : row_shift + out_rows,
                                    column_shift : column_shift + out_columns,
                                ]
                            )
                            kernels.append(down_weight[frame_tap, row_tap, column_tap].T)
                stacked = jnp.concatenate(windows, axis=-1)
                parity_parts.append(
                    jnp.dot(
                        stacked,
                        jnp.concatenate(kernels, axis=0),
                        preferred_element_type=jnp.float32,
                    )
                )
    alternated = jnp.stack(parity_parts).reshape(
        2, 2, 2, out_frames, out_rows, out_columns, channels
    )
    alternated = jnp.transpose(alternated, (3, 0, 4, 1, 5, 2, 6)).reshape(
        frames, height, columns, channels
    )
    grad_summed = alternated.astype(jnp.bfloat16)
    padded_g = row_margin(frame_edge(grad_summed, 2, -1))
    padded_g = jnp.pad(padded_g, ((0, 0), (0, 0), (1, 1), (0, 0)))
    grad_activated = jnp.zeros((frames, height, columns, channels), jnp.float32)
    block_pieces = []
    for frame_tap, row_tap in plane_list():
        window = jnp.concatenate(
            [
                padded_g[
                    2 - frame_tap : 2 - frame_tap + frames,
                    2 - row_tap : 2 - row_tap + height,
                    2 - column_tap : 2 - column_tap + columns,
                ]
                for column_tap in range(3)
            ],
            axis=-1,
        )
        flipped = jnp.concatenate(
            [block_weight[frame_tap, row_tap, column_tap].T for column_tap in range(3)], axis=0
        )
        grad_activated = grad_activated + jnp.dot(
            window, flipped, preferred_element_type=jnp.float32
        )
        forward_window = jnp.concatenate(
            [
                padded_a[
                    frame_tap : frame_tap + frames,
                    row_tap : row_tap + height,
                    column_tap : column_tap + columns,
                ]
                for column_tap in range(3)
            ],
            axis=-1,
        )
        block_pieces.append(outer_sum(forward_window, grad_summed))
    grad_block_term = jnp.concatenate(block_pieces, axis=0)
    sigmoid_value = jax.nn.sigmoid(source)
    grad_video = (
        grad_summed.astype(jnp.float32)
        + grad_activated * sigmoid_value * (1.0 + source * (1.0 - sigmoid_value))
    ).astype(jnp.bfloat16)
    grad_block, grad_down = lax.psum((grad_block_term, grad_down_term), ("dp", "rows", "tm"))
    total_cells = (
        frames
        * height
        * columns
        * lax.axis_size("dp")
        * lax.axis_size("rows")
        * lax.axis_size("tm")
    )
    grad_block = grad_block.reshape(3, 3, 3, channels, channels) * total_cells ** (-0.5)
    grad_down = grad_down.reshape(3, 3, 3, channels, wide_channels) * (total_cells / 8) ** (-0.5)
    return (latents[None], grad_video[None], grad_block, grad_down)


def solution(mesh):
    return jax.shard_map(
        local,
        mesh=mesh,
        in_specs=(P("dp", "tm", "rows", None, None), P(), P(), P("dp", "tm", "rows", None, None)),
        out_specs=(P("dp", "tm", "rows", None, None), P("dp", "tm", "rows", None, None), P(), P()),
        check_vma=False,
    )
```

profile of v0, /device:TPU:0, one launch (start us, length us, event | category | flops | bytes accessed | tf_op | source)
XLA Modules:
  0.0 352.5 jit_solution(12740241202639483197)
XLA Ops:
  9.8 6.3 %collective-permute-start = (bf16[2,4,128,128]{3,2,1,0:T(8,128)(2,1)S(1)}, bf16[2,4,128,128]{3,2,1,0:T(8,128)(2,1)}, u32[]{:S(2)}, u32[]{:S(2)}) collective-permute-start(bf16[2,4,128,128]{3,2,1,0:T(8,128)(2,1)S(1)} %fusion.93), channel_id=1, source_target_pairs={{0,1},{1,2},{2,3},{4,5},{5,6},{6,7},{8,9},{9,10},{10,11},{12,13},{... | collective-permute-start | bytes 786440 | tf_op jit(solution)/shard_map/ppermute | solution.py:10
  17.1 1.7 fusion.221
  21.6 1.6 copy.131
  23.2 1.6 copy.130
  26.3 1.6 copy.128
  27.9 1.6 copy.127
  29.4 1.6 copy.126
  31.0 1.6 copy.125
  42.9 1.6 copy.132
  47.9 1.6 copy.111
  49.4 1.6 copy.113
  51.0 1.6 copy.112
  52.6 1.6 copy.110
  56.3 1.6 copy.124
  59.4 1.6 copy.122
  61.0 1.6 copy.121
  62.6 1.6 copy.120
  65.7 1.6 copy.118
  67.3 1.6 copy.117
  68.9 1.6 copy.116
  70.4 1.6 copy.115
  80.5 1.6 pad_maximum_fusion.42
  82.1 4.3 %collective-permute-start.1 = (bf16[4,1,128,128]{3,2,1,0:T(8,128)(2,1)}, bf16[4,1,128,128]{3,2,1,0:T(8,128)(2,1)}, u32[]{:S(2)}, u32[]{:S(2)}) collective-permute-start(bf16[4,1,128,128]{3,2,1,0:T(8,128)(2,1)} %get-tuple-element.122), channel_id=1, source_target_pairs={{0,4},{1,5},{2,6},{3,7},{8,12},{9,13},{10,14},{11,15},{16,20},{17,... | collective-permute-start | bytes 393224 | tf_op jit(solution)/shard_map/ppermute | solution.py:21
  127.4 3.7 %collective-permute-start.8 = (bf16[4,1,128,128]{3,2,1,0:T(8,128)(2,1)S(1)}, bf16[4,1,128,128]{3,2,1,0:T(8,128)(2,1)S(1)}, u32[]{:S(2)}, u32[]{:S(2)}) collective-permute-start(bf16[4,1,128,128]{3,2,1,0:T(8,128)(2,1)S(1)} %get-tuple-element.118), channel_id=1, source_target_pairs={{0,4},{1,5},{2,6},{3,7},{8,12},{9,13},{10,14},{11,15},{16,20},{17,... | collective-permute-start | bytes 393224 | tf_op jit(solution)/shard_map/ppermute | solution.py:21
  144.1 4.5 %collective-permute-start.3 = (bf16[1,4,128,128]{3,2,1,0:T(8,128)(2,1)S(1)}, bf16[1,4,128,128]{3,2,1,0:T(8,128)(2,1)S(1)}, u32[]{:S(2)}, u32[]{:S(2)}) collective-permute-start(bf16[1,4,128,128]{3,2,1,0:T(8,128)(2,1)S(1)} %slice.757), channel_id=1, source_target_pairs={{0,1},{1,2},{2,3},{4,5},{5,6},{6,7},{8,9},{9,10},{10,11},{12,13},{... | collective-permute-start | bytes 393224 | tf_op jit(solution)/shard_map/ppermute | solution.py:10
  155.3 2.4 fusion.225
  157.7 2.8 collective-permute-start.4
  189.2 2.4 fusion.231
  191.8 1.6 fusion.227
  201.8 138.8 %all-reduce.7.cloned.1.call-done = (f32[3456,128]{1,0:T(8,128)}, f32[3456,256]{1,0:T(8,128)}) async-done(((f32[3456,128]{1,0:T(8,128)}, f32[3456,256]{1,0:T(8,128)}), (f32[3456,128]{1,0:T(8,128)}, f32[3456,256]{1,0:T(8,128)})) %all-reduce.7.cloned.1.call-update) | async-done | bytes 5308432 | tf_op jit(solution)/shard_map/psum | solution.py:199
  340.6 3.0 broadcast_multiply_fusion.1
  343.6 2.0 broadcast_multiply_fusion
  (327 shorter events, 132.1 us)
Async XLA Ops:
  7.2 11.7 %copy-start.2 = (bf16[3,3,3,128,128]{4,3,2,1,0:T(8,128)(2,1)S(1)}, bf16[3,3,3,128,128]{4,3,2,1,0:T(8,128)(2,1)}, u32[]{:S(2)}) copy-start(bf16[3,3,3,128,128]{4,3,2,1,0:T(8,128)(2,1)} %param.5) | copy-start | bytes 2654212
  7.2 333.4 %all-reduce.7.cloned.1.call-start = ((), (), s32[]{:S(2)}) async-start(), calls=%async_computation | async-start | bytes 10616832 | tf_op jit(solution)/shard_map/psum | solution.py:199
  7.2 37.2 %collective-permute-start.5 = (bf16[1,2,64,256]{3,2,1,0:T(8,128)(2,1)}, bf16[1,2,64,256]{3,2,1,0:T(8,128)(2,1)S(1)}, u32[]{:S(2)}, u32[]{:S(2)}) collective-permute-start(bf16[1,2,64,256]{3,2,1,0:T(8,128)(2,1)} %bitcast.459), channel_id=1, source_target_pairs={{1,0},{2,1},{3,2},{5,4},{6,5},{7,6},{9,8},{10,9},{11,10},{13,12},{... | collective-permute-start | bytes 196616 | tf_op jit(solution)/shard_map/ppermute | solution.py:10
  9.8 70.7 %collective-permute-start = (bf16[2,4,128,128]{3,2,1,0:T(8,128)(2,1)S(1)}, bf16[2,4,128,128]{3,2,1,0:T(8,128)(2,1)}, u32[]{:S(2)}, u32[]{:S(2)}) collective-permute-start(bf16[2,4,128,128]{3,2,1,0:T(8,128)(2,1)S(1)} %fusion.93), channel_id=1, source_target_pairs={{0,1},{1,2},{2,3},{4,5},{5,6},{6,7},{8,9},{9,10},{10,11},{12,13},{... | collective-permute-start | bytes 786440 | tf_op jit(solution)/shard_map/ppermute | solution.py:10
  18.8 1.7 copy-start
  21.6 22.9 %copy-start.4 = (bf16[1,1,2,64,256]{4,3,2,1,0:T(8,128)(2,1)S(1)}, bf16[1,1,2,64,256]{4,3,2,1,0:T(8,128)(2,1)}, u32[]{:S(2)}) copy-start(bf16[1,1,2,64,256]{4,3,2,1,0:T(8,128)(2,1)} %param.7) | copy-start | bytes 196612
  45.1 27.6 %collective-permute-start.6 = (bf16[2,1,64,256]{3,2,1,0:T(8,128)(2,1)}, bf16[2,1,64,256]{3,2,1,0:T(8,128)(2,1)}, u32[]{:S(2)}, u32[]{:S(2)}) collective-permute-start(bf16[2,1,64,256]{3,2,1,0:T(8,128)(2,1)} %pad_maximum_fusion.44), channel_id=1, source_target_pairs={{4,0},{5,1},{6,2},{7,3},{12,8},{13,9},{14,10},{15,11},{20,16},{21,... | collective-permute-start | bytes 196616 | tf_op jit(solution)/shard_map/ppermute | solution.py:10
  54.9 17.1 %copy-start.23 = (bf16[1,1,1,128,256]{4,3,2,1,0:T(8,128)(2,1)S(1)}, bf16[1,1,1,128,256]{4,3,2,1,0:T(8,128)(2,1)}, u32[]{:S(2)}) copy-start(bf16[1,1,1,128,256]{4,3,2,1,0:T(8,128)(2,1)} %get-tuple-element.24) | copy-start | bytes 196612
  73.6 2.5 copy-start.39
  73.6 2.5 copy-start.40
  73.6 2.5 copy-start.41
  73.6 2.5 copy-start.48
  73.8 2.6 copy-start.46
  73.8 2.6 copy-start.47
  73.9 2.8 copy-start.42
  73.9 2.8 copy-start.43
  73.9 2.8 copy-start.44
  73.9 2.8 copy-start.45
  79.2 48.2 %collective-permute-start.7 = (bf16[2,4,128,128]{3,2,1,0:T(8,128)(2,1)S(1)}, bf16[2,4,128,128]{3,2,1,0:T(8,128)(2,1)S(1)}, u32[]{:S(2)}, u32[]{:S(2)}) collective-permute-start(bf16[2,4,128,128]{3,2,1,0:T(8,128)(2,1)S(1)} %bitcast.440), channel_id=1, source_target_pairs={{1,0},{2,1},{3,2},{5,4},{6,5},{7,6},{9,8},{10,9},{11,10},{13,12},{... | collective-permute-start | bytes 786440 | tf_op jit(solution)/shard_map/ppermute | solution.py:10
  82.1 50.3 %collective-permute-start.1 = (bf16[4,1,128,128]{3,2,1,0:T(8,128)(2,1)}, bf16[4,1,128,128]{3,2,1,0:T(8,128)(2,1)}, u32[]{:S(2)}, u32[]{:S(2)}) collective-permute-start(bf16[4,1,128,128]{3,2,1,0:T(8,128)(2,1)} %get-tuple-element.122), channel_id=1, source_target_pairs={{0,4},{1,5},{2,6},{3,7},{8,12},{9,13},{10,14},{11,15},{16,20},{17,... | collective-permute-start | bytes 393224 | tf_op jit(solution)/shard_map/ppermute | solution.py:21
  86.4 46.0 %collective-permute-start.2 = (bf16[4,1,128,128]{3,2,1,0:T(8,128)(2,1)}, bf16[4,1,128,128]{3,2,1,0:T(8,128)(2,1)}, u32[]{:S(2)}, u32[]{:S(2)}) collective-permute-start(bf16[4,1,128,128]{3,2,1,0:T(8,128)(2,1)} %get-tuple-element.123), channel_id=1, source_target_pairs={{4,0},{5,1},{6,2},{7,3},{12,8},{13,9},{14,10},{15,11},{20,16},{21,... | collective-permute-start | bytes 393224 | tf_op jit(solution)/shard_map/ppermute | solution.py:23
  127.4 26.5 %collective-permute-start.8 = (bf16[4,1,128,128]{3,2,1,0:T(8,128)(2,1)S(1)}, bf16[4,1,128,128]{3,2,1,0:T(8,128)(2,1)S(1)}, u32[]{:S(2)}, u32[]{:S(2)}) collective-permute-start(bf16[4,1,128,128]{3,2,1,0:T(8,128)(2,1)S(1)} %get-tuple-element.118), channel_id=1, source_target_pairs={{0,4},{1,5},{2,6},{3,7},{8,12},{9,13},{10,14},{11,15},{16,20},{17,... | collective-permute-start | bytes 393224 | tf_op jit(solution)/shard_map/ppermute | solution.py:21
  131.1 24.0 %collective-permute-start.9 = (bf16[4,1,128,128]{3,2,1,0:T(8,128)(2,1)S(1)}, bf16[4,1,128,128]{3,2,1,0:T(8,128)(2,1)S(1)}, u32[]{:S(2)}, u32[]{:S(2)}) collective-permute-start(bf16[4,1,128,128]{3,2,1,0:T(8,128)(2,1)S(1)} %get-tuple-element.119), channel_id=1, source_target_pairs={{4,0},{5,1},{6,2},{7,3},{12,8},{13,9},{14,10},{15,11},{20,16},{21,... | collective-permute-start | bytes 393224 | tf_op jit(solution)/shard_map/ppermute | solution.py:23
  137.5 1.4 copy-start.32
  144.1 13.6 %collective-permute-start.3 = (bf16[1,4,128,128]{3,2,1,0:T(8,128)(2,1)S(1)}, bf16[1,4,128,128]{3,2,1,0:T(8,128)(2,1)S(1)}, u32[]{:S(2)}, u32[]{:S(2)}) collective-permute-start(bf16[1,4,128,128]{3,2,1,0:T(8,128)(2,1)S(1)} %slice.757), channel_id=1, source_target_pairs={{0,1},{1,2},{2,3},{4,5},{5,6},{6,7},{8,9},{9,10},{10,11},{12,13},{... | collective-permute-start | bytes 393224 | tf_op jit(solution)/shard_map/ppermute | solution.py:10
  157.7 3.9 %collective-permute-start.4 = (bf16[3,1,128,128]{3,2,1,0:T(8,128)(2,1)S(1)}, bf16[3,1,128,128]{3,2,1,0:T(8,128)(2,1)S(1)}, u32[]{:S(2)}, u32[]{:S(2)}) collective-permute-start(bf16[3,1,128,128]{3,2,1,0:T(8,128)(2,1)S(1)} %pad_maximum_fusion.43), channel_id=1, source_target_pairs={{0,4},{1,5},{2,6},{3,7},{8,12},{9,13},{10,14},{11,15},{16,20},{17,... | collective-permute-start | bytes 294920 | tf_op jit(solution)/shard_map/ppermute | solution.py:10
  191.7 1.7 copy-start.21
  191.7 1.7 copy-start.22
  191.7 1.7 copy-start.67
  191.7 1.7 copy-start.69
  191.8 1.7 copy-start.70
  340.6 3.0 copy-start.1
  (55 other events, 57.2 us)
Sparse Core Ops, SparseCore 0:
  191.8 148.7 all-reduce.6
where the time goes:
time: 358 us; the launch traced here: 352 us
  waiting for transfers between devices  139 us (39%)
  local copies, waits for them, and re-layouts  133 us (37%)
  starting transfers between devices  28.1 us (8%)
  matrix products  23.9 us (7%)
  between operations  15.4 us (4%)
  other arithmetic  13.4 us (4%)
    psum x1, waiting for transfers between devices, local(): lax.psum((grad_block_term, grad_down_term), ('dp', 'rows', 'tm'))  139 us
    unnamed x245, local copies, waits for them, and re-layouts  107 us
    ppermute x6, starting transfers between devices, from_behind(): lax.ppermute(value, axis, [(source, source + steps) for source in range(l...  17.5 us
    slice x27, local copies, waits for them, and re-layouts, local(): padded_b[frame_tap:frame_tap + frames - 1:2, row_tap:row_tap + height - 1...  13.3 us
    dot_general x10, matrix products, outer_sum(): lax.dot_general(patches.reshape(-1, patches.shape[-1]), cotangent_part.re...  8.07 us
    ppermute x2, starting transfers between devices, with_halo(): lax.ppermute(tail, axis, [(i, (i + 1) % count) for i in range(ends)])  8.01 us
  transfers between devices with their start and end apart: 11, of which 1 were waited for; matrix products, arithmetic and copies ran while one was open for 36% of the time, Pallas kernels for 0%

commit v1 on v0

v1 whole, which is shorter than its diff:
```python
import functools

import jax
import jax.numpy as jnp
from jax import lax
from jax.experimental import pallas as pl
from jax.experimental.pallas import tpu as pltpu
from jax.sharding import PartitionSpec as P

BF = jnp.bfloat16
F32 = jnp.float32
MESH = pl.DeviceIdType.MESH
SPLIT = 41


def shifted(value, axis, steps):
    count = lax.axis_size(axis)
    pairs = [(i, i + steps) for i in range(count) if 0 <= i + steps < count]
    return lax.ppermute(value, axis, pairs)


def before(x):
    rolled = pltpu.roll(x, 1, axis=x.ndim - 2)
    index = lax.broadcasted_iota(jnp.int32, x.shape, x.ndim - 2)
    return jnp.where(index == 0, 0.0, rolled)


def after(x):
    size = x.shape[-2]
    rolled = pltpu.roll(x, size - 1, axis=x.ndim - 2)
    index = lax.broadcasted_iota(jnp.int32, x.shape, x.ndim - 2)
    return jnp.where(index == size - 1, 0.0, rolled)


def nn(x, y):
    return lax.dot_general(x, y, (((1,), (0,)), ((), ())), preferred_element_type=F32)


def nt(x, y):
    return lax.dot_general(x, y, (((1,), (1,)), ((), ())), preferred_element_type=F32)


def flat(x):
    return x.reshape(-1, x.shape[-1])


def put(g_ref, k, value):
    stream, at = (0, k) if k < SPLIT else (1, k - SPLIT)
    g_ref[stream, at * 8 : at * 8 + 8] = value.reshape(8, 16, 128)


def compute_kernel(v_ref, c_ref, bw_ref, dw_ref, lat_ref, gv_ref, g_ref, a4, s4, g4, c2, w4, bt, dt):
    c = 128
    inner = (lax.axis_index("rows") > 0).astype(F32)
    zero = jnp.zeros((c, c), BF)
    units = g_ref.shape[1]
    g_ref[0, SPLIT * 8 :] = jnp.zeros((units - SPLIT * 8, 16, 128), F32)
    g_ref[1, (81 - SPLIT) * 8 :] = jnp.zeros((units - (81 - SPLIT) * 8, 16, 128), F32)
    planes = [(a, b) for a in range(3) for b in range(3)]
    for k, (a, b) in enumerate(planes):
        w = [bw_ref[a, b, i] for i in range(3)]
        d = [dw_ref[a, b, i] for i in range(3)]
        for i in range(3):
            w4[k, i * c : i * c + c, 0:c] = w[i]
            w4[k, (i + 1) * c : (i + 2) * c, c:] = w[i]
            bt[k, 0:c, (2 - i) * c : (3 - i) * c] = w[i]
            bt[k, c:, (3 - i) * c : (4 - i) * c] = w[i]
        w4[k, 3 * c :, 0:c] = zero
        w4[k, 0:c, c:] = zero
        bt[k, 0:c, 3 * c :] = zero
        bt[k, c:, 0:c] = zero
        dt[k, 0:c, 0 : 2 * c] = d[1]
        dt[k, c:, 0 : 2 * c] = d[2]
        dt[k, c:, 2 * c :] = d[0]
        dt[k, 0:c, 2 * c :] = jnp.zeros((c, 2 * c), BF)
    for t in range(3):
        cot = c_ref[t]
        c2[t, :, :, 0 : 2 * c] = cot
        c2[t, :, :, 2 * c :] = after(cot.astype(F32)).astype(BF)
    frame_sets = {0: [(1, 0)], 1: [(0, 1), (2, 0)]}
    row_sets = {0: [(1, 1)], 1: [(0, 1), (2, 0)]}
    for fp in range(2):
        for rp in range(2):
            total = None
            for a, t in frame_sets[fp]:
                for b, i in row_sets[rp]:
                    term = nt(flat(c2[t : t + 2, i : i + 3]), dt[a * 3 + b])
                    total = term if total is None else total + term
            gs = total.astype(BF).reshape(2, 3, 64, 2 * c).astype(F32)
            low = before(gs[..., c:])
            high = after(gs[..., :c])
            for h in range(2):
                for r in range(3):
                    keep = inner if (rp == 1 and r == 0) else None
                    row = jnp.concatenate([low[h, r], gs[h, r], high[h, r]], axis=-1)
                    if keep is not None:
                        row = row * keep
                    g4[2 * h + fp, 2 * r + (1 - rp)] = row.astype(BF)
    for f in range(5):
        v = v_ref[f].astype(F32)
        act = (v / (1.0 + jnp.exp(-v))).astype(BF).astype(F32)
        a4[f, :, :, 0:c] = before(act[..., c:]).astype(BF)
        a4[f, :, :, c : 3 * c] = act.astype(BF)
        a4[f, :, :, 3 * c :] = after(act[..., :c]).astype(BF)
    own_t = flat(a4[3:5, 2:6, :, c : 3 * c]).astype(F32).T.astype(BF)
    grad_act = None
    for k, (a, b) in enumerate(planes):
        window = flat(g4[2 - a : 4 - a, 2 - b : 6 - b])
        term = nt(window, bt[k])
        grad_act = term if grad_act is None else grad_act + term
        outer = nn(own_t, window)
        even, odd = outer[:c], outer[c:]
        put(g_ref, k * 3 + 2, even[:, 0:c] + odd[:, c : 2 * c])
        put(g_ref, k * 3 + 1, even[:, c : 2 * c] + odd[:, 2 * c : 3 * c])
        put(g_ref, k * 3, even[:, 2 * c : 3 * c] + odd[:, 3 * c :])
    v = flat(v_ref[3:5, 2:6]).astype(F32)
    sig = 1.0 / (1.0 + jnp.exp(-v))
    own_g = flat(g4[0:2, 1:5, :, c : 3 * c]).astype(F32)
    gv = own_g + grad_act * sig * (1.0 + v * (1.0 - sig))
    gv_ref[...] = gv.astype(BF).reshape(2, 4, 64, 2 * c)
    branch = None
    for k, (a, b) in enumerate(planes):
        term = nn(flat(a4[a : a + 3, b : b + 5]), w4[k])
        branch = term if branch is None else branch + term
    branch = branch.reshape(3, 5, 64, 2 * c)
    for f in range(3):
        for r in range(5):
            row = (v_ref[f + 2, r + 1].astype(F32) + branch[f, r]).astype(BF).astype(F32)
            if r == 0:
                row = row * inner
            s4[f, r, :, 0:c] = before(row[:, c:]).astype(BF)
            s4[f, r, :, c:] = row.astype(BF)
    latents = None
    for a, b in planes:
        lhs = jnp.concatenate([s4[a, b], s4[a, b + 2]], axis=0)
        term = nn(lhs, dw_ref[a, b].reshape(3 * c, 2 * c))
        latents = term if latents is None else latents + term
    lat_ref[...] = latents.astype(BF).reshape(1, 2, 64, 2 * c)
    turned = {}
    for s in range(2):
        for p in range(2):
            pair = jnp.concatenate([s4[s + 1, p + 1, :, c:], s4[s + 1, p + 3, :, c:]], axis=0)
            turned[s, p] = pair.astype(F32).T.astype(BF)
    frame_map = [(1, 1), (0, 0), (1, 0)]
    row_map = [(1, 2), (0, 1), (1, 1)]
    for k, (a, b) in enumerate(planes):
        (s, t), (p, i) = frame_map[a], row_map[b]
        outer = nn(turned[s, p], flat(c2[t, i : i + 2]))
        parts = [outer[c:, 2 * c :], outer[:c, : 2 * c], outer[c:, : 2 * c]]
        for tap in range(3):
            at = 27 + (k * 3 + tap) * 2
            put(g_ref, at, parts[tap][:, :c])
            put(g_ref, at + 1, parts[tap][:, c:])


def stage_lists(rows, dp, tm):
    row_stage = ("rows", 1, rows)
    if dp == 4:
        return [
            [row_stage, ("dp", 1, 2), ("dp", 2, 2), ("tm", 1, tm)],
            [row_stage, ("dp", 2, 2), ("dp", 1, 2), ("tm", 1, tm)],
        ]
    return [[row_stage, ("dp", 1, dp), ("tm", 1, tm)]] * 2


def member(stage):
    axis, step, count = stage
    return lax.rem(lax.axis_index(axis) // step, count)


def peer(stage, ahead):
    axis, step, count = stage
    mine = member(stage)
    other = lax.rem(mine + ahead, count)
    return other, {axis: lax.axis_index(axis) + (other - mine) * step}


def reduce_kernel(lists, copies, scales, x_ref, out_ref, acc, send, recv, load_sem, send_sem, recv_sem):
    units = acc.shape[1]
    barrier = pltpu.get_barrier_semaphore()
    greeted = 0
    for stage in lists[0]:
        for ahead in range(1, stage[2]):
            _, device = peer(stage, ahead)
            pl.semaphore_signal(barrier, inc=1, device_id=device, device_id_type=MESH)
            greeted += 1
    load = pltpu.make_async_copy(x_ref, acc, load_sem)
    load.start()
    load.wait()
    pl.semaphore_wait(barrier, greeted)

    offsets = [0, 0]
    lengths = [units, units]
    history = [[], []]
    slots = [0, 0]
    sems = [0, 0]
    pending = []

    def chunks(length):
        step = max(k for k in range(1, 12) if length % k == 0)
        return length // step, step

    def start(s, k):
        stage = lists[s][k]
        count = stage[2]
        piece = lengths[s] // count
        started = []
        for ahead in range(1, count):
            other, device = peer(stage, ahead)
            base = offsets[s] + other * piece
            loops, step = chunks(piece)

            @pl.loop(0, loops)
            def _(n, base=base, step=step):
                at = pl.ds(base + n * step, step)
                send[s, at] = acc[s, at].astype(BF)

            slot = pl.ds(slots[s], piece)
            copy = pltpu.make_async_remote_copy(
                src_ref=send.at[s, pl.ds(base, piece)],
                dst_ref=recv.at[s, slot],
                send_sem=send_sem.at[s, sems[s]],
                recv_sem=recv_sem.at[s, sems[s]],
                device_id=device,
                device_id_type=MESH,
            )
            copy.start()
            started.append((copy, slots[s]))
            slots[s] += piece
            sems[s] += 1
        history[s].append((offsets[s], lengths[s]))
        offsets[s] = offsets[s] + member(stage) * piece
        lengths[s] = piece
        return started

    def finish(s, started):
        loops, step = chunks(lengths[s])
        base = offsets[s]
        for copy, slot in started:
            copy.wait_recv()
            pending.append(copy)

        @pl.loop(0, loops)
        def _(n):
            at = pl.ds(base + n * step, step)
            value = acc[s, at]
            for _, slot in started:
                value = value + recv[s, pl.ds(slot + n * step, step)].astype(F32)
            acc[s, at] = value

    def spread(s, k):
        stage = lists[s][k]
        started = []
        for ahead in range(1, stage[2]):
            _, device = peer(stage, ahead)
            at = pl.ds(offsets[s], lengths[s])
            copy = pltpu.make_async_remote_copy(
                src_ref=out_ref.at[s, at],
                dst_ref=out_ref.at[s, at],
                send_sem=send_sem.at[s, sems[s]],
                recv_sem=recv_sem.at[s, sems[s]],
                device_id=device,
                device_id_type=MESH,
            )
            copy.start()
            started.append(copy)
            sems[s] += 1
        offsets[s], lengths[s] = history[s][k]
        return started

    last = len(lists[0]) - 1
    flying = [start(s, 0) for s in range(2)]
    for k in range(last + 1):
        for s in range(2):
            finish(s, flying[s])
            if k < last:
                flying[s] = start(s, k + 1)
            else:
                tile = lax.broadcasted_iota(jnp.int32, (lengths[s], 16, 128), 0) + offsets[s]
                value = acc[s, pl.ds(offsets[s], lengths[s])]
                first = scales[0] if s == 0 else scales[1]
                scaled = value * jnp.where(tile < 27 * 8, first, scales[1])
                out_ref[s, pl.ds(offsets[s], lengths[s])] = scaled.astype(BF)
                flying[s] = spread(s, last)
    for k in range(last, -1, -1):
        for s in range(2):
            for copy in flying[s]:
                copy.wait_recv()
                pending.append(copy)
            if k > 0:
                flying[s] = spread(s, k - 1)
    for copy in pending:
        copy.wait_send()


def local(video_cells, block_weight, down_weight, cotangent):
    frames, height, columns, channels = video_cells.shape[1:]
    wide = down_weight.shape[-1]
    dp, rows, tm = (lax.axis_size(name) for name in ("dp", "rows", "tm"))
    devices = dp * rows * tm
    video = video_cells[0].reshape(frames, height, columns // 2, 2 * channels)
    cot = cotangent[0]
    video_x = jnp.concatenate([shifted(video[1:], "tm", 2), shifted(video, "tm", 1), video], axis=0)
    video_x = jnp.concatenate(
        [shifted(video_x[:, height - 2 :], "rows", 1), video_x, shifted(video_x[:, :1], "rows", -1)], axis=1
    )
    cot_x = jnp.concatenate([cot, shifted(cot, "tm", -1), shifted(cot, "tm", -2)], axis=0)
    cot_x = jnp.concatenate(
        [shifted(cot_x[:, 1:], "rows", 1), cot_x, shifted(cot_x[:, :1], "rows", -1)], axis=1
    )
    unit = -(-SPLIT * 8 // devices)
    units = unit * devices
    vmem = pl.BlockSpec(memory_space=pltpu.VMEM)
    latents, grad_video, terms = pl.pallas_call(
        compute_kernel,
        out_shape=(
            jax.ShapeDtypeStruct((1, 2, 64, 256), BF),
            jax.ShapeDtypeStruct((2, 4, 64, 256), BF),
            jax.ShapeDtypeStruct((2, units, 16, 128), F32),
        ),
        in_specs=[vmem] * 4,
        out_specs=(vmem,) * 3,
        scratch_shapes=[
            pltpu.VMEM((5, 7, 64, 512), BF),
            pltpu.VMEM((3, 5, 64, 384), BF),
            pltpu.VMEM((4, 6, 64, 512), BF),
            pltpu.VMEM((3, 4, 64, 512), BF),
            pltpu.VMEM((9, 512, 256), BF),
            pltpu.VMEM((9, 256, 512), BF),
            pltpu.VMEM((9, 256, 512), BF),
        ],
        compiler_params=pltpu.CompilerParams(vmem_limit_bytes=56 * 1024 * 1024),
        name="conv_parts",
    )(video_x, cot_x, block_weight, down_weight)
    lists = stage_lists(rows, dp, tm)
    copies = sum(stage[2] - 1 for stage in lists[0])
    slots, length = 0, units
    for stage in lists[0]:
        length //= stage[2]
        slots += (stage[2] - 1) * length
    cells = frames * height * columns * devices
    scales = (float(cells) ** -0.5, float(cells / 8) ** -0.5)
    summed = pl.pallas_call(
        functools.partial(reduce_kernel, lists, copies, scales),
        out_shape=jax.ShapeDtypeStruct((2, units, 16, 128), BF),
        in_specs=[pl.BlockSpec(memory_space=pl.ANY)],
        out_specs=vmem,
        scratch_shapes=[
            pltpu.VMEM((2, units, 16, 128), F32),
            pltpu.VMEM((2, units, 16, 128), BF),
            pltpu.VMEM((2, slots, 16, 128), BF),
            pltpu.SemaphoreType.DMA,
            pltpu.SemaphoreType.DMA((2, 2 * copies)),
            pltpu.SemaphoreType.DMA((2, 2 * copies)),
        ],
        compiler_params=pltpu.CompilerParams(
            collective_id=0, has_side_effects=True, vmem_limit_bytes=32 * 1024 * 1024
        ),
        name="sum_parts",
    )(terms)
    grad_block = summed[0, : 27 * 8].astype(F32).reshape(3, 3, 3, channels, channels)
    down = jnp.concatenate(
        [summed[0, 27 * 8 : SPLIT * 8], summed[1, : (81 - SPLIT) * 8]], axis=0
    ).reshape(3, 3, 3, 2, channels, wide // 2)
    grad_down = jnp.concatenate([down[:, :, :, 0], down[:, :, :, 1]], axis=-1).astype(F32)
    return (
        latents.reshape(1, frames // 2, height // 2, columns // 2, wide),
        grad_video.reshape(1, frames, height, columns, channels),
        grad_block,
        grad_down,
    )


def solution(mesh):
    return jax.shard_map(
        local,
        mesh=mesh,
        in_specs=(P("dp", "tm", "rows", None, None), P(), P(), P("dp", "tm", "rows", None, None)),
        out_specs=(P("dp", "tm", "rows", None, None), P("dp", "tm", "rows", None, None), P(), P()),
        check_vma=False,
    )
```

time: 358 us -> 108 us (0.30); the launches traced: 352 us -> 107 us
  waiting for transfers between devices: 139 us -> 2.8 us
  local copies, waits for them, and re-layouts: 133 us -> 6.65 us
  Pallas kernels: 0 us -> 72 us
  matrix products: 23.9 us -> 0 us
  between operations: 15.4 us -> 0.85 us
  starting transfers between devices: 28.1 us -> 18.4 us
  other arithmetic: 13.4 us -> 6.41 us
    psum x1 -> x0, waiting for transfers between devices: 139 us -> none  [local(): lax.psum((grad_block_term, grad_down_term), ('dp', 'rows', 'tm'))]
    unnamed x245 -> x8, local copies, waits for them, and re-layouts: 107 us -> 3.22 us
    pallas_call x0 -> x2, Pallas kernels: none -> 72 us  [the longest x1 57.4 us: local(): pl.pallas_call(functools.partial(reduce_kernel, lists, copies, scales), o...]
    dot_general x37 -> x0, matrix products: 23.9 us -> none  [the longest x10 8.07 us: outer_sum(): lax.dot_general(patches.reshape(-1, patches.shape[-1]), cotangent_part.re...]
    slice x37 -> x6, local copies, waits for them, and re-layouts: 23.7 us -> 1.17 us  [the longest x2 0.97 us: local(): video[1:]]
    ppermute x10 -> x8, starting transfers between devices: 28.1 us -> 18.4 us  [shifted(): return lax.ppermute(value, axis, pairs)]
    mul x2 -> x0, other arithmetic: 5.01 us -> none  [the longest x1 2.98 us: local(): grad_block.reshape(3, 3, 3, channels, channels) * total_cells ** (-0.5)]
  transfers between devices with their start and end apart: 11 -> 8, of which waited for: 1 -> 3; matrix products, arithmetic and copies ran while one was open for 36% -> 3% of each run, Pallas kernels for 0% -> 0%
where the time goes in v1:
time: 108 us; the launch traced here: 107 us
  Pallas kernels  72 us (67%)
  starting transfers between devices  18.4 us (17%)
  local copies, waits for them, and re-layouts  6.65 us (6%)
  other arithmetic  6.41 us (6%)
  waiting for transfers between devices  2.8 us (3%)
    pallas_call x1, Pallas kernels, local(): pl.pallas_call(functools.partial(reduce_kernel, lists, copies, scales), o...  57.4 us
    ppermute x8, starting transfers between devices, shifted(): return lax.ppermute(value, axis, pairs)  18.4 us
    pallas_call x1, Pallas kernels, local(): pl.pallas_call(compute_kernel, out_shape=(jax.ShapeDtypeStruct((1, 2, 64,...  14.6 us
    unnamed x8, local copies, waits for them, and re-layouts  3.22 us
    ppermute x8, waiting for transfers between devices, shifted(): return lax.ppermute(value, axis, pairs)  2.8 us
  transfers between devices with their start and end apart: 8, of which 3 were waited for; matrix products, arithmetic and copies ran while one was open for 3% of the time, Pallas kernels for 0%

profile of v1, /device:TPU:0, one launch (start us, length us, event | category | flops | bytes accessed | tf_op | source)
XLA Modules:
  0.0 107.1 jit_solution(5626254644685598323)
XLA Ops:
  0.6 1.3 %collective-permute-start.5 = (bf16[1,2,64,256]{3,2,1,0:T(8,128)(2,1)}, bf16[1,2,64,256]{3,2,1,0:T(8,128)(2,1)S(1)}, u32[]{:S(2)}, u32[]{:S(2)}) collective-permute-start(bf16[1,2,64,256]{3,2,1,0:T(8,128)(2,1)} %bitcast.25), channel_id=1, source_target_pairs={{2,0},{3,1},{6,4},{7,5},{10,8},{11,9},{14,12},{15,13},{18,16},{19,... | collective-permute-start | bytes 196616 | tf_op jit(solution)/shard_map/ppermute | solution.py:19
  1.9 1.3 %collective-permute-start.4 = (bf16[1,2,64,256]{3,2,1,0:T(8,128)(2,1)}, bf16[1,2,64,256]{3,2,1,0:T(8,128)(2,1)S(1)}, u32[]{:S(2)}, u32[]{:S(2)}) collective-permute-start(bf16[1,2,64,256]{3,2,1,0:T(8,128)(2,1)} %bitcast.26), channel_id=1, source_target_pairs={{1,0},{2,1},{3,2},{5,4},{6,5},{7,6},{9,8},{10,9},{11,10},{13,12},{... | collective-permute-start | bytes 196616 | tf_op jit(solution)/shard_map/ppermute | solution.py:19
  3.2 1.0 reshape_squeeze.3
  4.3 0.0 copy-start.2
  4.3 5.7 %collective-permute-start.1 = (bf16[2,4,64,256]{3,2,1,0:T(8,128)(2,1)S(1)}, bf16[2,4,64,256]{3,2,1,0:T(8,128)(2,1)S(1)}, u32[]{:S(2)}, u32[]{:S(2)}) collective-permute-start(bf16[2,4,64,256]{3,2,1,0:T(8,128)(2,1)S(1)} %reshape_squeeze.3), channel_id=1, source_target_pairs={{0,1},{1,2},{2,3},{4,5},{5,6},{6,7},{8,9},{9,10},{10,11},{12,13},{... | collective-permute-start | bytes 786440 | tf_op jit(solution)/shard_map/ppermute | solution.py:19
  10.0 0.9 slice.33
  11.0 4.9 %collective-permute-start = (bf16[1,4,64,256]{3,2,1,0:T(8,128)(2,1)S(1)}, bf16[1,4,64,256]{3,2,1,0:T(8,128)(2,1)S(1)}, u32[]{:S(2)}, u32[]{:S(2)}) collective-permute-start(bf16[1,4,64,256]{3,2,1,0:T(8,128)(2,1)S(1)} %slice.34), channel_id=1, source_target_pairs={{0,2},{1,3},{4,6},{5,7},{8,10},{9,11},{12,14},{13,15},{16,18},{17,... | collective-permute-start | bytes 393224 | tf_op jit(solution)/shard_map/ppermute | solution.py:19
  15.9 0.0 collective-permute-done.5
  16.0 0.9 pad_maximum_fusion.3
  16.8 1.6 %collective-permute-done = bf16[1,4,64,256]{3,2,1,0:T(8,128)(2,1)S(1)} collective-permute-done((bf16[1,4,64,256]{3,2,1,0:T(8,128)(2,1)S(1)}, bf16[1,4,64,256]{3,2,1,0:T(8,128)(2,1)S(1)}, u32[]{:S(2)}, u32[]{:S(2)}) %collective-permute-start) | collective-permute-done | bytes 131104 | tf_op jit(solution)/shard_map/ppermute | solution.py:19
  18.4 0.0 collective-permute-done.1
  18.5 1.3 %collective-permute-start.2 = (bf16[5,2,64,256]{3,2,1,0:T(8,128)(2,1)S(1)}, bf16[5,2,64,256]{3,2,1,0:T(8,128)(2,1)S(1)}, u32[]{:S(2)}, u32[]{:S(2)}) collective-permute-start(bf16[5,2,64,256]{3,2,1,0:T(8,128)(2,1)S(1)} %slice.44), channel_id=1, source_target_pairs={{0,4},{1,5},{2,6},{3,7},{8,12},{9,13},{10,14},{11,15},{16,20},{17,... | collective-permute-start | bytes 983048 | tf_op jit(solution)/shard_map/ppermute | solution.py:19
  19.9 1.3 %collective-permute-start.6 = (bf16[3,1,64,256]{3,2,1,0:T(8,128)(2,1)S(1)}, bf16[3,1,64,256]{3,2,1,0:T(8,128)(2,1)S(1)}, u32[]{:S(2)}, u32[]{:S(2)}) collective-permute-start(bf16[3,1,64,256]{3,2,1,0:T(8,128)(2,1)S(1)} %get-tuple-element.12), channel_id=1, source_target_pairs={{0,4},{1,5},{2,6},{3,7},{8,12},{9,13},{10,14},{11,15},{16,20},{17,... | collective-permute-start | bytes 294920 | tf_op jit(solution)/shard_map/ppermute | solution.py:19
  21.2 1.3 %collective-permute-start.7 = (bf16[3,1,64,256]{3,2,1,0:T(8,128)(2,1)S(1)}, bf16[3,1,64,256]{3,2,1,0:T(8,128)(2,1)S(1)}, u32[]{:S(2)}, u32[]{:S(2)}) collective-permute-start(bf16[3,1,64,256]{3,2,1,0:T(8,128)(2,1)S(1)} %get-tuple-element.13), channel_id=1, source_target_pairs={{4,0},{5,1},{6,2},{7,3},{12,8},{13,9},{14,10},{15,11},{20,16},{21,... | collective-permute-start | bytes 294920 | tf_op jit(solution)/shard_map/ppermute | solution.py:19
  22.5 1.3 %collective-permute-start.3 = (bf16[5,1,64,256]{3,2,1,0:T(8,128)(2,1)S(1)}, bf16[5,1,64,256]{3,2,1,0:T(8,128)(2,1)S(1)}, u32[]{:S(2)}, u32[]{:S(2)}) collective-permute-start(bf16[5,1,64,256]{3,2,1,0:T(8,128)(2,1)S(1)} %slice.45), channel_id=1, source_target_pairs={{4,0},{5,1},{6,2},{7,3},{12,8},{13,9},{14,10},{15,11},{20,16},{21,... | collective-permute-start | bytes 491528 | tf_op jit(solution)/shard_map/ppermute | solution.py:19
  23.8 0.6 collective-permute-done.7
  24.4 0.8 pad_maximum_fusion.2.c_ref
  25.2 0.6 collective-permute-done.3
  25.8 0.0 collective-permute-done.2
  25.8 1.1 %pad_maximum_fusion.1.v_ref = bf16[5,7,64,256]{3,2,1,0:T(8,128)(2,1)} fusion(bf16[5,1,64,256]{3,2,1,0:T(8,128)(2,1)S(1)} %collective-permute-done.3, bf16[5,4,64,256]{3,2,1,0:T(8,128)(2,1)S(1)} %constant_dynamic-update-slice_fusion, bf16[5,2,64,256]{3,2,1,0:T(8,128)(2,1)S(1)} %collective-permute-done.2), kind=kLoop, calls=%fused_computation.3 | loop fusion | flops 1146880 | bytes 2293760 | tf_op jit(solution)/shard_map/concatenate | solution.py:304
  26.9 14.6 %conv_parts.1 = (bf16[1,2,64,256]{3,2,1,0:T(8,128)(2,1)}, bf16[2,4,64,256]{3,2,1,0:T(8,128)(2,1)}, f32[2,352,16,128]{3,2,1,0:T(8,128)}) custom-call(bf16[5,7,64,256]{3,2,1,0:T(8,128)(2,1)} %pad_maximum_fusion.1.v_ref, bf16[3,4,64,256]{3,2,1,0:T(8,128)(2,1)} %pad_maximum_fusion.2.c_ref, bf16[3,3,3,128,128]{4,3,2,1,0:T(8,128)(2,1)} %bw_ref.1, ...), custom_call_target="tpu_custom_call" | custom-call | tf_op jit(solution)/shard_map/conv_parts/pallas_call | solution.py:314
  41.6 2.6 %copy-done = f32[2,352,16,128]{3,2,1,0:T(8,128)S(1)} copy-done((f32[2,352,16,128]{3,2,1,0:T(8,128)S(1)}, f32[2,352,16,128]{3,2,1,0:T(8,128)}, u32[]{:S(2)}) %copy-start) | copy-done | bytes 5767192
  44.2 57.4 %sum_parts.1 = bf16[2,352,16,128]{3,2,1,0:T(8,128)(2,1)S(1)} custom-call(f32[2,352,16,128]{3,2,1,0:T(8,128)S(1)} %copy-done), custom_call_target="tpu_custom_call" | custom-call | tf_op jit(solution)/shard_map/sum_parts/pallas_call | solution.py:343
  101.6 0.0 copy-start.1
  101.6 0.2 slice.39
  101.8 0.2 slice_bitcast_fusion
  102.0 0.5 copy-done.1
  102.6 0.8 reshape.23
  103.4 0.2 pad_maximum_fusion
  103.5 0.2 slice_bitcast_fusion.2
  103.7 1.4 %convert.1 = f32[3,3,3,128,128]{4,3,2,1,0:T(8,128)} convert(bf16[3,3,3,128,128]{4,3,2,1,0:T(8,128)(2,1)S(1)} %bitcast.24) | non-fusion elementwise | flops 442368 | bytes 2654208 | tf_op jit(solution)/shard_map/convert_element_type | solution.py:361
  105.1 2.0 %maximum_convert_fusion = f32[3,3,3,128,256]{4,3,2,1,0:T(8,128)} fusion(bf16[3,3,3,128,128]{4,3,2,1,0:T(8,128)(2,1)S(1)} %get-tuple-element.11, bf16[3,3,3,128,128]{4,3,2,1,0:T(8,128)(2,1)S(1)} %get-tuple-element.10), kind=kLoop, calls=%fused_computation.1 | loop fusion | flops 3538944 | bytes 5308416 | tf_op jit(solution)/shard_map/convert_element_type | solution.py:365
  (12 shorter events, 0.2 us)
Async XLA Ops:
  0.6 15.3 %collective-permute-start.5 = (bf16[1,2,64,256]{3,2,1,0:T(8,128)(2,1)}, bf16[1,2,64,256]{3,2,1,0:T(8,128)(2,1)S(1)}, u32[]{:S(2)}, u32[]{:S(2)}) collective-permute-start(bf16[1,2,64,256]{3,2,1,0:T(8,128)(2,1)} %bitcast.25), channel_id=1, source_target_pairs={{2,0},{3,1},{6,4},{7,5},{10,8},{11,9},{14,12},{15,13},{18,16},{19,... | collective-permute-start | bytes 196616 | tf_op jit(solution)/shard_map/ppermute | solution.py:19
  1.9 14.0 %collective-permute-start.4 = (bf16[1,2,64,256]{3,2,1,0:T(8,128)(2,1)}, bf16[1,2,64,256]{3,2,1,0:T(8,128)(2,1)S(1)}, u32[]{:S(2)}, u32[]{:S(2)}) collective-permute-start(bf16[1,2,64,256]{3,2,1,0:T(8,128)(2,1)} %bitcast.26), channel_id=1, source_target_pairs={{1,0},{2,1},{3,2},{5,4},{6,5},{7,6},{9,8},{10,9},{11,10},{13,12},{... | collective-permute-start | bytes 196616 | tf_op jit(solution)/shard_map/ppermute | solution.py:19
  4.3 20.1 %copy-start.2 = (bf16[1,1,2,64,256]{4,3,2,1,0:T(8,128)(2,1)S(1)}, bf16[1,1,2,64,256]{4,3,2,1,0:T(8,128)(2,1)}, u32[]{:S(2)}) copy-start(bf16[1,1,2,64,256]{4,3,2,1,0:T(8,128)(2,1)} %param.7) | copy-start | bytes 196612
  4.3 14.2 %collective-permute-start.1 = (bf16[2,4,64,256]{3,2,1,0:T(8,128)(2,1)S(1)}, bf16[2,4,64,256]{3,2,1,0:T(8,128)(2,1)S(1)}, u32[]{:S(2)}, u32[]{:S(2)}) collective-permute-start(bf16[2,4,64,256]{3,2,1,0:T(8,128)(2,1)S(1)} %reshape_squeeze.3), channel_id=1, source_target_pairs={{0,1},{1,2},{2,3},{4,5},{5,6},{6,7},{8,9},{9,10},{10,11},{12,13},{... | collective-permute-start | bytes 786440 | tf_op jit(solution)/shard_map/ppermute | solution.py:19
  11.0 7.4 %collective-permute-start = (bf16[1,4,64,256]{3,2,1,0:T(8,128)(2,1)S(1)}, bf16[1,4,64,256]{3,2,1,0:T(8,128)(2,1)S(1)}, u32[]{:S(2)}, u32[]{:S(2)}) collective-permute-start(bf16[1,4,64,256]{3,2,1,0:T(8,128)(2,1)S(1)} %slice.34), channel_id=1, source_target_pairs={{0,2},{1,3},{4,6},{5,7},{8,10},{9,11},{12,14},{13,15},{16,18},{17,... | collective-permute-start | bytes 393224 | tf_op jit(solution)/shard_map/ppermute | solution.py:19
  18.5 7.3 %collective-permute-start.2 = (bf16[5,2,64,256]{3,2,1,0:T(8,128)(2,1)S(1)}, bf16[5,2,64,256]{3,2,1,0:T(8,128)(2,1)S(1)}, u32[]{:S(2)}, u32[]{:S(2)}) collective-permute-start(bf16[5,2,64,256]{3,2,1,0:T(8,128)(2,1)S(1)} %slice.44), channel_id=1, source_target_pairs={{0,4},{1,5},{2,6},{3,7},{8,12},{9,13},{10,14},{11,15},{16,20},{17,... | collective-permute-start | bytes 983048 | tf_op jit(solution)/shard_map/ppermute | solution.py:19
  19.9 3.9 %collective-permute-start.6 = (bf16[3,1,64,256]{3,2,1,0:T(8,128)(2,1)S(1)}, bf16[3,1,64,256]{3,2,1,0:T(8,128)(2,1)S(1)}, u32[]{:S(2)}, u32[]{:S(2)}) collective-permute-start(bf16[3,1,64,256]{3,2,1,0:T(8,128)(2,1)S(1)} %get-tuple-element.12), channel_id=1, source_target_pairs={{0,4},{1,5},{2,6},{3,7},{8,12},{9,13},{10,14},{11,15},{16,20},{17,... | collective-permute-start | bytes 294920 | tf_op jit(solution)/shard_map/ppermute | solution.py:19
  21.2 3.2 %collective-permute-start.7 = (bf16[3,1,64,256]{3,2,1,0:T(8,128)(2,1)S(1)}, bf16[3,1,64,256]{3,2,1,0:T(8,128)(2,1)S(1)}, u32[]{:S(2)}, u32[]{:S(2)}) collective-permute-start(bf16[3,1,64,256]{3,2,1,0:T(8,128)(2,1)S(1)} %get-tuple-element.13), channel_id=1, source_target_pairs={{4,0},{5,1},{6,2},{7,3},{12,8},{13,9},{14,10},{15,11},{20,16},{21,... | collective-permute-start | bytes 294920 | tf_op jit(solution)/shard_map/ppermute | solution.py:19
  22.5 3.3 %collective-permute-start.3 = (bf16[5,1,64,256]{3,2,1,0:T(8,128)(2,1)S(1)}, bf16[5,1,64,256]{3,2,1,0:T(8,128)(2,1)S(1)}, u32[]{:S(2)}, u32[]{:S(2)}) collective-permute-start(bf16[5,1,64,256]{3,2,1,0:T(8,128)(2,1)S(1)} %slice.45), channel_id=1, source_target_pairs={{4,0},{5,1},{6,2},{7,3},{12,8},{13,9},{14,10},{15,11},{20,16},{21,... | collective-permute-start | bytes 491528 | tf_op jit(solution)/shard_map/ppermute | solution.py:19
  41.6 2.6 %copy-start = (f32[2,352,16,128]{3,2,1,0:T(8,128)S(1)}, f32[2,352,16,128]{3,2,1,0:T(8,128)}, u32[]{:S(2)}) copy-start(f32[2,352,16,128]{3,2,1,0:T(8,128)} %get-tuple-element.9.x_ref) | copy-start | bytes 17301508
  101.6 1.0 copy-start.1

commit v2 on v1

--- a/solution.py
+++ b/solution.py
@@ -175,7 +175,7 @@
     return other, {axis: lax.axis_index(axis) + (other - mine) * step}
 
 
-def reduce_kernel(lists, copies, scales, x_ref, out_ref, acc, send, recv, load_sem, send_sem, recv_sem):
+def reduce_kernel(lists, copies, scales, x_ref, out_ref, acc, send, recv, send_sem, recv_sem):
     units = acc.shape[1]
     barrier = pltpu.get_barrier_semaphore()
     greeted = 0
@@ -184,9 +184,6 @@
             _, device = peer(stage, ahead)
             pl.semaphore_signal(barrier, inc=1, device_id=device, device_id_type=MESH)
             greeted += 1
-    load = pltpu.make_async_copy(x_ref, acc, load_sem)
-    load.start()
-    load.wait()
     pl.semaphore_wait(barrier, greeted)
 
     offsets = [0, 0]
@@ -202,6 +199,7 @@
 
     def start(s, k):
         stage = lists[s][k]
+        source = x_ref if k == 0 else acc
         count = stage[2]
         piece = lengths[s] // count
         started = []
@@ -213,7 +211,7 @@
             @pl.loop(0, loops)
             def _(n, base=base, step=step):
                 at = pl.ds(base + n * step, step)
-                send[s, at] = acc[s, at].astype(BF)
+                send[s, at] = source[s, at].astype(BF)
 
             slot = pl.ds(slots[s], piece)
             copy = pltpu.make_async_remote_copy(
@@ -233,7 +231,8 @@
         lengths[s] = piece
         return started
 
-    def finish(s, started):
+    def finish(s, k, started):
+        source = x_ref if k == 0 else acc
         loops, step = chunks(lengths[s])
         base = offsets[s]
         for copy, slot in started:
@@ -243,7 +242,7 @@
         @pl.loop(0, loops)
         def _(n):
             at = pl.ds(base + n * step, step)
-            value = acc[s, at]
+            value = source[s, at]
             for _, slot in started:
                 value = value + recv[s, pl.ds(slot + n * step, step)].astype(F32)
             acc[s, at] = value
@@ -272,7 +271,7 @@
     flying = [start(s, 0) for s in range(2)]
     for k in range(last + 1):
         for s in range(2):
-            finish(s, flying[s])
+            finish(s, k, flying[s])
             if k < last:
                 flying[s] = start(s, k + 1)
             else:
@@ -329,7 +328,7 @@
             pltpu.VMEM((9, 256, 512), BF),
             pltpu.VMEM((9, 256, 512), BF),
         ],
-        compiler_params=pltpu.CompilerParams(vmem_limit_bytes=56 * 1024 * 1024),
+        compiler_params=pltpu.CompilerParams(vmem_limit_bytes=32 * 1024 * 1024),
         name="conv_parts",
     )(video_x, cot_x, block_weight, down_weight)
     lists = stage_lists(rows, dp, tm)
@@ -343,13 +342,12 @@
     summed = pl.pallas_call(
         functools.partial(reduce_kernel, lists, copies, scales),
         out_shape=jax.ShapeDtypeStruct((2, units, 16, 128), BF),
-        in_specs=[pl.BlockSpec(memory_space=pl.ANY)],
+        in_specs=[vmem],
         out_specs=vmem,
         scratch_shapes=[
             pltpu.VMEM((2, units, 16, 128), F32),
             pltpu.VMEM((2, units, 16, 128), BF),
             pltpu.VMEM((2, slots, 16, 128), BF),
-            pltpu.SemaphoreType.DMA,
             pltpu.SemaphoreType.DMA((2, 2 * copies)),
             pltpu.SemaphoreType.DMA((2, 2 * copies)),
         ],

time: 108 us -> 99 us (0.917)
  Pallas kernels: 72 us -> 67.5 us
  local copies, waits for them, and re-layouts: 6.65 us -> 3.48 us
  other arithmetic: 6.41 us -> 4.66 us
    pallas_call x1, Pallas kernels: 14.6 us -> 9.93 us  [local(): pl.pallas_call(compute_kernel, out_shape=(jax.ShapeDtypeStruct((1, 2, 64,...]
    unnamed x8, local copies, waits for them, and re-layouts: 3.22 us -> 0.05 us
where the time goes in v2:
time: 99 us; the launch traced here: 98.6 us
  Pallas kernels  67.5 us (68%)
  starting transfers between devices  18.6 us (19%)
  other arithmetic  4.66 us (5%)
  waiting for transfers between devices  3.54 us (4%)
  local copies, waits for them, and re-layouts  3.48 us (4%)
    pallas_call x1, Pallas kernels, local(): pl.pallas_call(functools.partial(reduce_kernel, lists, copies, scales), o...  57.5 us
    ppermute x8, starting transfers between devices, shifted(): return lax.ppermute(value, axis, pairs)  18.6 us
    pallas_call x1, Pallas kernels, local(): pl.pallas_call(compute_kernel, out_shape=(jax.ShapeDtypeStruct((1, 2, 64,...  9.93 us
    ppermute x8, waiting for transfers between devices, shifted(): return lax.ppermute(value, axis, pairs)  3.54 us
    convert_element_type x1, other arithmetic, local(): jnp.concatenate([down[:, :, :, 0], down[:, :, :, 1]], axis=-1).astype(F32)  2.04 us
  transfers between devices with their start and end apart: 8, of which 3 were waited for; matrix products, arithmetic and copies ran while one was open for 3% of the time, Pallas kernels for 0%

profile of v2, /device:TPU:0, one launch (start us, length us, event | category | flops | bytes accessed | tf_op | source)
XLA Modules:
  0.0 98.6 jit_solution(14979061847526455182)
XLA Ops:
  0.6 1.3 %collective-permute-start.5 = (bf16[1,2,64,256]{3,2,1,0:T(8,128)(2,1)}, bf16[1,2,64,256]{3,2,1,0:T(8,128)(2,1)S(1)}, u32[]{:S(2)}, u32[]{:S(2)}) collective-permute-start(bf16[1,2,64,256]{3,2,1,0:T(8,128)(2,1)} %bitcast.25), channel_id=1, source_target_pairs={{2,0},{3,1},{6,4},{7,5},{10,8},{11,9},{14,12},{15,13},{18,16},{19,... | collective-permute-start | bytes 196616 | tf_op jit(solution)/shard_map/ppermute | solution.py:19
  1.9 1.3 %collective-permute-start.4 = (bf16[1,2,64,256]{3,2,1,0:T(8,128)(2,1)}, bf16[1,2,64,256]{3,2,1,0:T(8,128)(2,1)S(1)}, u32[]{:S(2)}, u32[]{:S(2)}) collective-permute-start(bf16[1,2,64,256]{3,2,1,0:T(8,128)(2,1)} %bitcast.26), channel_id=1, source_target_pairs={{1,0},{2,1},{3,2},{5,4},{6,5},{7,6},{9,8},{10,9},{11,10},{13,12},{... | collective-permute-start | bytes 196616 | tf_op jit(solution)/shard_map/ppermute | solution.py:19
  3.2 1.0 %reshape_squeeze.3 = bf16[2,4,64,256]{3,2,1,0:T(8,128)(2,1)S(1)} reshape(bf16[1,2,4,128,128]{4,3,2,1,0:T(8,128)(2,1)} %param.4) | data formatting | bytes 524288 | tf_op jit(solution)/shard_map/reshape;squeeze | solution.py:300
  4.3 0.0 copy-start.2
  4.3 5.7 %collective-permute-start.1 = (bf16[2,4,64,256]{3,2,1,0:T(8,128)(2,1)S(1)}, bf16[2,4,64,256]{3,2,1,0:T(8,128)(2,1)S(1)}, u32[]{:S(2)}, u32[]{:S(2)}) collective-permute-start(bf16[2,4,64,256]{3,2,1,0:T(8,128)(2,1)S(1)} %reshape_squeeze.3), channel_id=1, source_target_pairs={{0,1},{1,2},{2,3},{4,5},{5,6},{6,7},{8,9},{9,10},{10,11},{12,13},{... | collective-permute-start | bytes 786440 | tf_op jit(solution)/shard_map/ppermute | solution.py:19
  10.0 0.9 slice.33
  11.0 4.9 %collective-permute-start = (bf16[1,4,64,256]{3,2,1,0:T(8,128)(2,1)S(1)}, bf16[1,4,64,256]{3,2,1,0:T(8,128)(2,1)S(1)}, u32[]{:S(2)}, u32[]{:S(2)}) collective-permute-start(bf16[1,4,64,256]{3,2,1,0:T(8,128)(2,1)S(1)} %slice.34), channel_id=1, source_target_pairs={{0,2},{1,3},{4,6},{5,7},{8,10},{9,11},{12,14},{13,15},{16,18},{17,... | collective-permute-start | bytes 393224 | tf_op jit(solution)/shard_map/ppermute | solution.py:19
  15.9 0.0 collective-permute-done.5
  16.0 0.0 collective-permute-done.4
  16.0 0.9 pad_maximum_fusion.3
  16.8 1.6 %collective-permute-done = bf16[1,4,64,256]{3,2,1,0:T(8,128)(2,1)S(1)} collective-permute-done((bf16[1,4,64,256]{3,2,1,0:T(8,128)(2,1)S(1)}, bf16[1,4,64,256]{3,2,1,0:T(8,128)(2,1)S(1)}, u32[]{:S(2)}, u32[]{:S(2)}) %collective-permute-start) | collective-permute-done | bytes 131104 | tf_op jit(solution)/shard_map/ppermute | solution.py:19
  18.4 0.0 collective-permute-done.1
  18.5 1.3 %collective-permute-start.2 = (bf16[5,2,64,256]{3,2,1,0:T(8,128)(2,1)S(1)}, bf16[5,2,64,256]{3,2,1,0:T(8,128)(2,1)S(1)}, u32[]{:S(2)}, u32[]{:S(2)}) collective-permute-start(bf16[5,2,64,256]{3,2,1,0:T(8,128)(2,1)S(1)} %slice.44), channel_id=1, source_target_pairs={{0,4},{1,5},{2,6},{3,7},{8,12},{9,13},{10,14},{11,15},{16,20},{17,... | collective-permute-start | bytes 983048 | tf_op jit(solution)/shard_map/ppermute | solution.py:19
  19.9 0.0 copy-start
  19.9 0.0 copy-start.1
  19.9 1.4 %collective-permute-start.6 = (bf16[3,1,64,256]{3,2,1,0:T(8,128)(2,1)S(1)}, bf16[3,1,64,256]{3,2,1,0:T(8,128)(2,1)S(1)}, u32[]{:S(2)}, u32[]{:S(2)}) collective-permute-start(bf16[3,1,64,256]{3,2,1,0:T(8,128)(2,1)S(1)} %get-tuple-element.12), channel_id=1, source_target_pairs={{0,4},{1,5},{2,6},{3,7},{8,12},{9,13},{10,14},{11,15},{16,20},{17,... | collective-permute-start | bytes 294920 | tf_op jit(solution)/shard_map/ppermute | solution.py:19
  21.3 1.3 %collective-permute-start.7 = (bf16[3,1,64,256]{3,2,1,0:T(8,128)(2,1)S(1)}, bf16[3,1,64,256]{3,2,1,0:T(8,128)(2,1)S(1)}, u32[]{:S(2)}, u32[]{:S(2)}) collective-permute-start(bf16[3,1,64,256]{3,2,1,0:T(8,128)(2,1)S(1)} %get-tuple-element.13), channel_id=1, source_target_pairs={{4,0},{5,1},{6,2},{7,3},{12,8},{13,9},{14,10},{15,11},{20,16},{21,... | collective-permute-start | bytes 294920 | tf_op jit(solution)/shard_map/ppermute | solution.py:19
  22.7 1.3 %collective-permute-start.3 = (bf16[5,1,64,256]{3,2,1,0:T(8,128)(2,1)S(1)}, bf16[5,1,64,256]{3,2,1,0:T(8,128)(2,1)S(1)}, u32[]{:S(2)}, u32[]{:S(2)}) collective-permute-start(bf16[5,1,64,256]{3,2,1,0:T(8,128)(2,1)S(1)} %slice.45), channel_id=1, source_target_pairs={{4,0},{5,1},{6,2},{7,3},{12,8},{13,9},{14,10},{15,11},{20,16},{21,... | collective-permute-start | bytes 491528 | tf_op jit(solution)/shard_map/ppermute | solution.py:19
  24.0 0.6 collective-permute-done.7
  24.5 0.1 pad_maximum_fusion.2.c_ref
  24.6 1.4 %collective-permute-done.3 = bf16[5,1,64,256]{3,2,1,0:T(8,128)(2,1)S(1)} collective-permute-done((bf16[5,1,64,256]{3,2,1,0:T(8,128)(2,1)S(1)}, bf16[5,1,64,256]{3,2,1,0:T(8,128)(2,1)S(1)}, u32[]{:S(2)}, u32[]{:S(2)}) %collective-permute-start.3) | collective-permute-done | bytes 163872 | tf_op jit(solution)/shard_map/ppermute | solution.py:19
  26.0 0.0 collective-permute-done.2
  26.0 0.1 pad_maximum_fusion.1.v_ref
  26.1 9.9 %conv_parts.1 = (bf16[1,2,64,256]{3,2,1,0:T(8,128)(2,1)}, bf16[2,4,64,256]{3,2,1,0:T(8,128)(2,1)S(1)}, f32[2,352,16,128]{3,2,1,0:T(8,128)S(1)}) custom-call(bf16[5,7,64,256]{3,2,1,0:T(8,128)(2,1)S(1)} %pad_maximum_fusion.1.v_ref, bf16[3,4,64,256]{3,2,1,0:T(8,128)(2,1)S(1)} %pad_maximum_fusion.2.c_ref, bf16[3,3,3,128,128]{4,3,2,1,0:T(8,128)(2,1)S(1)} %copy-done.1, ...), custom_call_target="tpu_custom_call" | custom-call | tf_op jit(solution)/shard_map/conv_parts/pallas_call | solution.py:313
  36.1 57.5 %sum_parts.1 = bf16[2,352,16,128]{3,2,1,0:T(8,128)(2,1)S(1)} custom-call(f32[2,352,16,128]{3,2,1,0:T(8,128)S(1)} %get-tuple-element.9.x_ref), custom_call_target="tpu_custom_call" | custom-call | tf_op jit(solution)/shard_map/sum_parts/pallas_call | solution.py:342
  93.6 0.2 slice.39
  93.8 0.2 slice_bitcast_fusion
  94.0 0.8 reshape.23
  94.8 0.2 pad_maximum_fusion
  95.0 0.2 slice_bitcast_fusion.2
  95.1 1.4 %convert.1 = f32[3,3,3,128,128]{4,3,2,1,0:T(8,128)} convert(bf16[3,3,3,128,128]{4,3,2,1,0:T(8,128)(2,1)S(1)} %bitcast.24) | non-fusion elementwise | flops 442368 | bytes 2654208 | tf_op jit(solution)/shard_map/convert_element_type | solution.py:359
  96.5 2.0 %maximum_convert_fusion = f32[3,3,3,128,256]{4,3,2,1,0:T(8,128)} fusion(bf16[3,3,3,128,128]{4,3,2,1,0:T(8,128)(2,1)S(1)} %get-tuple-element.11, bf16[3,3,3,128,128]{4,3,2,1,0:T(8,128)(2,1)S(1)} %get-tuple-element.10), kind=kLoop, calls=%fused_computation.1 | loop fusion | flops 3538944 | bytes 5308416 | tf_op jit(solution)/shard_map/convert_element_type | solution.py:363
  (12 shorter events, 0.2 us)
Async XLA Ops:
  0.6 15.3 %collective-permute-start.5 = (bf16[1,2,64,256]{3,2,1,0:T(8,128)(2,1)}, bf16[1,2,64,256]{3,2,1,0:T(8,128)(2,1)S(1)}, u32[]{:S(2)}, u32[]{:S(2)}) collective-permute-start(bf16[1,2,64,256]{3,2,1,0:T(8,128)(2,1)} %bitcast.25), channel_id=1, source_target_pairs={{2,0},{3,1},{6,4},{7,5},{10,8},{11,9},{14,12},{15,13},{18,16},{19,... | collective-permute-start | bytes 196616 | tf_op jit(solution)/shard_map/ppermute | solution.py:19
  1.9 14.0 %collective-permute-start.4 = (bf16[1,2,64,256]{3,2,1,0:T(8,128)(2,1)}, bf16[1,2,64,256]{3,2,1,0:T(8,128)(2,1)S(1)}, u32[]{:S(2)}, u32[]{:S(2)}) collective-permute-start(bf16[1,2,64,256]{3,2,1,0:T(8,128)(2,1)} %bitcast.26), channel_id=1, source_target_pairs={{1,0},{2,1},{3,2},{5,4},{6,5},{7,6},{9,8},{10,9},{11,10},{13,12},{... | collective-permute-start | bytes 196616 | tf_op jit(solution)/shard_map/ppermute | solution.py:19
  4.3 20.3 %copy-start.2 = (bf16[1,1,2,64,256]{4,3,2,1,0:T(8,128)(2,1)S(1)}, bf16[1,1,2,64,256]{4,3,2,1,0:T(8,128)(2,1)}, u32[]{:S(2)}) copy-start(bf16[1,1,2,64,256]{4,3,2,1,0:T(8,128)(2,1)} %param.7) | copy-start | bytes 196612
  4.3 14.2 %collective-permute-start.1 = (bf16[2,4,64,256]{3,2,1,0:T(8,128)(2,1)S(1)}, bf16[2,4,64,256]{3,2,1,0:T(8,128)(2,1)S(1)}, u32[]{:S(2)}, u32[]{:S(2)}) collective-permute-start(bf16[2,4,64,256]{3,2,1,0:T(8,128)(2,1)S(1)} %reshape_squeeze.3), channel_id=1, source_target_pairs={{0,1},{1,2},{2,3},{4,5},{5,6},{6,7},{8,9},{9,10},{10,11},{12,13},{... | collective-permute-start | bytes 786440 | tf_op jit(solution)/shard_map/ppermute | solution.py:19
  11.0 7.4 %collective-permute-start = (bf16[1,4,64,256]{3,2,1,0:T(8,128)(2,1)S(1)}, bf16[1,4,64,256]{3,2,1,0:T(8,128)(2,1)S(1)}, u32[]{:S(2)}, u32[]{:S(2)}) collective-permute-start(bf16[1,4,64,256]{3,2,1,0:T(8,128)(2,1)S(1)} %slice.34), channel_id=1, source_target_pairs={{0,2},{1,3},{4,6},{5,7},{8,10},{9,11},{12,14},{13,15},{16,18},{17,... | collective-permute-start | bytes 393224 | tf_op jit(solution)/shard_map/ppermute | solution.py:19
  18.5 7.4 %collective-permute-start.2 = (bf16[5,2,64,256]{3,2,1,0:T(8,128)(2,1)S(1)}, bf16[5,2,64,256]{3,2,1,0:T(8,128)(2,1)S(1)}, u32[]{:S(2)}, u32[]{:S(2)}) collective-permute-start(bf16[5,2,64,256]{3,2,1,0:T(8,128)(2,1)S(1)} %slice.44), channel_id=1, source_target_pairs={{0,4},{1,5},{2,6},{3,7},{8,12},{9,13},{10,14},{11,15},{16,20},{17,... | collective-permute-start | bytes 983048 | tf_op jit(solution)/shard_map/ppermute | solution.py:19
  19.9 6.2 %copy-start = (bf16[3,3,3,128,256]{4,3,2,1,0:T(8,128)(2,1)S(1)}, bf16[3,3,3,128,256]{4,3,2,1,0:T(8,128)(2,1)}, u32[]{:S(2)}) copy-start(bf16[3,3,3,128,256]{4,3,2,1,0:T(8,128)(2,1)} %dw_ref.1) | copy-start | bytes 5308420
  19.9 6.2 %copy-start.1 = (bf16[3,3,3,128,128]{4,3,2,1,0:T(8,128)(2,1)S(1)}, bf16[3,3,3,128,128]{4,3,2,1,0:T(8,128)(2,1)}, u32[]{:S(2)}) copy-start(bf16[3,3,3,128,128]{4,3,2,1,0:T(8,128)(2,1)} %bw_ref.1) | copy-start | bytes 2654212
  19.9 4.1 %collective-permute-start.6 = (bf16[3,1,64,256]{3,2,1,0:T(8,128)(2,1)S(1)}, bf16[3,1,64,256]{3,2,1,0:T(8,128)(2,1)S(1)}, u32[]{:S(2)}, u32[]{:S(2)}) collective-permute-start(bf16[3,1,64,256]{3,2,1,0:T(8,128)(2,1)S(1)} %get-tuple-element.12), channel_id=1, source_target_pairs={{0,4},{1,5},{2,6},{3,7},{8,12},{9,13},{10,14},{11,15},{16,20},{17,... | collective-permute-start | bytes 294920 | tf_op jit(solution)/shard_map/ppermute | solution.py:19
  21.3 3.2 %collective-permute-start.7 = (bf16[3,1,64,256]{3,2,1,0:T(8,128)(2,1)S(1)}, bf16[3,1,64,256]{3,2,1,0:T(8,128)(2,1)S(1)}, u32[]{:S(2)}, u32[]{:S(2)}) collective-permute-start(bf16[3,1,64,256]{3,2,1,0:T(8,128)(2,1)S(1)} %get-tuple-element.13), channel_id=1, source_target_pairs={{4,0},{5,1},{6,2},{7,3},{12,8},{13,9},{14,10},{15,11},{20,16},{21,... | collective-permute-start | bytes 294920 | tf_op jit(solution)/shard_map/ppermute | solution.py:19
  22.7 3.3 %collective-permute-start.3 = (bf16[5,1,64,256]{3,2,1,0:T(8,128)(2,1)S(1)}, bf16[5,1,64,256]{3,2,1,0:T(8,128)(2,1)S(1)}, u32[]{:S(2)}, u32[]{:S(2)}) collective-permute-start(bf16[5,1,64,256]{3,2,1,0:T(8,128)(2,1)S(1)} %slice.45), channel_id=1, source_target_pairs={{4,0},{5,1},{6,2},{7,3},{12,8},{13,9},{14,10},{15,11},{20,16},{21,... | collective-permute-start | bytes 491528 | tf_op jit(solution)/shard_map/ppermute | solution.py:19
